TPU v7x, 32 devices: a whole 2x2x4 slice. The times are simulated.
32 devices in a mesh: cam: 4 (over y, core), tile: 8 (over z, x).
Axes of the slice: x: 2, y: 2, z: 4, core: 2. Of those that a mesh axis runs over, the one named last changes fastest.
Arguments:
- tokens: bfloat16 [5632, 1024], P(('cam', 'tile')), may hold values from -16 to 16
- ln_gain: float32 [1024], replicated, may hold values from 0.25 to 1.75
- gate_weight: bfloat16 [1024, 2730], P(('cam', 'tile')), may hold values from -0.1875 to 0.1875
- up_weight: bfloat16 [1024, 2730], P(('cam', 'tile')), may hold values from -0.1875 to 0.1875
- down_weight: bfloat16 [2730, 1024], P(None, ('cam', 'tile')), may hold values from -0.109375 to 0.109375
- head_gain: float32 [1024], replicated, may hold values from 0.25 to 1.75
- depth_weight: bfloat16 [1024, 64], replicated, may hold values from -24 to 24
- context_weight: bfloat16 [1024, 128], replicated, may hold values from -3 to 3
- slot_point: int32 [32, 8, 2503], P(('cam', 'tile')), may hold values from 0 to 11263, as said below
- slot_cell: int32 [32, 8, 2503], P(('cam', 'tile')), may hold values from 0 to 2047
- slot_count: int32 [32, 8], P(('cam', 'tile')), may hold values from 312 to 2503
- conv1_weight: bfloat16 [3, 3, 128, 128], replicated, may hold values from -0.1875 to 0.1875
- conv1_bias: float32 [128], replicated, may hold values from -1.5 to 1.5
- conv2_weight: bfloat16 [3, 3, 128, 128], replicated, may hold values from -0.1875 to 0.1875
- conv2_bias: float32 [128], replicated, may hold values from -1.5 to 1.5
Outputs:
- bev_out: bfloat16 [8, 32, 256, 128], P('cam', 'tile')
Inputs may be any that keep to these rules, and one draw needn't show every extreme that they name: slot_point[s, d, k] is a point of source s; the live slots (k < slot_count[s, d]) of one source name distinct points.
All inputs are finite; a program needn't handle non-finite values.
Results may differ from a plain program's by a relative error of at most 0.013.
The roundings to bfloat16 on the way count: a program that leaves them out, or rounds other values in their place, can miss the bound.
Values may be sent and summed in bfloat16 or wider, within the bound.
A program may use at most 64 MiB of HBM per device.

v0:
```python
import jax
import jax.numpy as jnp
from jax import lax
from jax.sharding import PartitionSpec as P

ROWS_DEV = 4
GRID_W = 256
SCN = 2


def extended_2(value, sides, width):
    for axis, dim in sides:
        size, length = (lax.axis_size(axis), value.shape[dim])
        up = [(i, (i + 1) % size) for i in range(size - 1)]
        down = [(j, i) for i, j in up]
        last = lax.slice_in_dim(value, length - width, length, axis=dim)
        leading = lax.slice_in_dim(value, 0, width, axis=dim)
        before = lax.ppermute(last, axis, up)
        after = lax.ppermute(leading, axis, down)
        value = jnp.concatenate([before, value, after], axis=dim)
    return value


def layer_norm(values, gain):
    center = values - jnp.mean(values, axis=-1, keepdims=True)
    spread = jnp.mean(center * center, axis=-1, keepdims=True)
    return center * lax.rsqrt(spread + 1e-06) * gain


def conv_rows(extended, weight):
    scenes = extended.shape[0]
    out_rows = extended.shape[1] - 2
    columns = extended.shape[2]
    padded = jnp.pad(extended, ((0, 0), (0, 0), (1, 1), (0, 0)))
    total = jnp.zeros((scenes * out_rows * columns, weight.shape[3]), jnp.float32)
    for row_shift in range(3):
        for col_shift in range(3):
            window = padded[:, row_shift : row_shift + out_rows, col_shift : col_shift + columns, :]
            window = window.reshape(-1, weight.shape[2])
            total = total + jnp.dot(
                window, weight[row_shift, col_shift], preferred_element_type=jnp.float32
            )
    return total.reshape(scenes, out_rows, columns, weight.shape[3])


def on_device(
    tokens,
    ln_gain,
    gate_weight,
    up_weight,
    down_weight,
    head_gain,
    depth_weight,
    context_weight,
    slot_point,
    slot_cell,
    slot_count,
    conv1_weight,
    conv1_bias,
    conv2_weight,
    conv2_bias,
):
    inputs = tokens.astype(jnp.float32)
    normed = layer_norm(inputs, ln_gain).astype(jnp.bfloat16)
    token_count = tokens.shape[0]
    gate_whole, up_whole = (
        lax.all_gather(gate_weight, ("cam", "tile"), axis=0, tiled=True),
        lax.all_gather(up_weight, ("cam", "tile"), axis=0, tiled=True),
    )
    gate_full = jnp.dot(normed, gate_whole, preferred_element_type=jnp.float32)
    up_full = jnp.dot(normed, up_whole, preferred_element_type=jnp.float32)
    hidden = (jax.nn.silu(gate_full) * up_full).astype(jnp.bfloat16)
    down_whole = lax.all_gather(down_weight, ("cam", "tile"), axis=1, tiled=True)
    branch_out = jnp.dot(hidden, down_whole, preferred_element_type=jnp.float32)
    updated = inputs + branch_out
    head_input = layer_norm(updated, head_gain).astype(jnp.bfloat16)
    logits = jnp.dot(head_input, depth_weight, preferred_element_type=jnp.float32)
    context = jnp.dot(head_input, context_weight, preferred_element_type=jnp.float32).astype(
        jnp.bfloat16
    )
    depth = jax.nn.softmax(logits, axis=-1)
    tiles = lax.axis_size("tile")
    slots = slot_point.shape[2]
    bins_count = depth.shape[1]
    channels = context.shape[1]
    slot_index = jnp.arange(slots, dtype=jnp.int32)[None, :]
    context_all = lax.all_gather(context, "tile", axis=0, tiled=True)
    own_points = slot_point.reshape(tiles, slots)
    live = (slot_index < slot_count.reshape(tiles, 1)).reshape(-1)
    weight_live = jnp.where(live, depth.reshape(-1)[own_points.reshape(-1)], 0.0).reshape(
        tiles, slots
    )
    got_weight = lax.all_to_all(
        weight_live.astype(jnp.bfloat16), "tile", split_axis=0, concat_axis=0, tiled=True
    ).astype(weight_live.dtype)
    got_tokens, got_cells = (
        lax.all_to_all(own_points // bins_count, "tile", split_axis=0, concat_axis=0, tiled=True),
        lax.all_to_all(
            slot_cell.reshape(tiles, slots), "tile", split_axis=0, concat_axis=0, tiled=True
        ),
    )
    cell_count = SCN * ROWS_DEV * GRID_W
    batch = 4
    rounds = tiles // batch
    batch_tokens = batch * token_count
    token_offset = jnp.arange(batch, dtype=jnp.int32)[:, None] * token_count
    weight_blocks = got_weight.reshape(rounds, batch * slots)
    token_blocks = (got_tokens.reshape(rounds, batch, slots) + token_offset[None]).reshape(
        rounds, batch * slots
    )
    cell_blocks = got_cells.reshape(rounds, batch * slots)
    context_blocks = context_all.reshape(rounds, batch_tokens, channels)

    def splat_step(total, pieces):
        weight_row, token_row, cell_row, context_rows = pieces
        spread_flat = jnp.zeros((cell_count * batch_tokens,), jnp.float32)
        spread_flat = spread_flat.at[cell_row * batch_tokens + token_row].add(weight_row)
        spread_table = spread_flat.reshape(cell_count, batch_tokens)
        total = total + jnp.dot(
            spread_table, context_rows.astype(jnp.float32), precision=lax.Precision.HIGHEST
        )
        return (total, None)

    splat, unused = lax.scan(
        splat_step,
        jnp.zeros((cell_count, channels), jnp.float32),
        (weight_blocks, token_blocks, cell_blocks, context_blocks),
    )
    bev = splat.astype(jnp.bfloat16).reshape(SCN, ROWS_DEV, GRID_W, channels)
    extended = extended_2(bev, (("tile", 1),), 2)
    middle_wide = jnp.maximum(conv_rows(extended, conv1_weight) + conv1_bias, 0.0)
    global_rows = lax.axis_index("tile") * ROWS_DEV - 1 + jnp.arange(ROWS_DEV + 2, dtype=jnp.int32)
    inside = (global_rows >= 0) & (global_rows < tiles * ROWS_DEV)
    middle_ext = jnp.where(inside[None, :, None, None], middle_wide, 0.0).astype(jnp.bfloat16)
    result = bev.astype(jnp.float32) + conv_rows(middle_ext, conv2_weight) + conv2_bias
    return result.astype(jnp.bfloat16)


def solution(mesh):
    return jax.shard_map(
        on_device,
        mesh=mesh,
        in_specs=(
            P(("cam", "tile"), None),
            P(),
            P(("cam", "tile"), None),
            P(("cam", "tile"), None),
            P(None, ("cam", "tile")),
            P(),
            P(),
            P(),
            P(("cam", "tile"), None, None),
            P(("cam", "tile"), None, None),
            P(("cam", "tile"), None),
            P(),
            P(),
            P(),
            P(),
        ),
        out_specs=P("cam", "tile", None, None),
        check_vma=False,
    )
```

profile of v0, /device:TPU:0, one launch (start us, length us, event | category | flops | bytes accessed | tf_op | source)
XLA Modules:
  0.0 551.0 jit_solution(15539689167989606263)
XLA Ops:
  8.8 1.9 and_select_fusion
  10.6 7.3 %all-to-all-start.1 = ((s32[8,1,2503]{2,1,0:T(1,128)}), s32[8,1,2503]{2,1,0:T(1,128)S(1)}, u32[]{:S(2)}, u32[]{:S(2)}) async-start(s32[8,1,2503]{2,1,0:T(1,128)} %and_select_fusion), calls=%async_computation.1 | async-start | bytes 163840 | tf_op jit(solution)/shard_map/all_to_all | solution.py:97
  21.5 3.5 all-to-all-done.1
  25.0 3.4 all-to-all-start
  28.8 6.9 %all-to-all-done = s32[8,1,2503]{2,1,0:T(1,128)S(1)} async-done(((s32[8,1,2503]{2,1,0:T(1,128)}), s32[8,1,2503]{2,1,0:T(1,128)S(1)}, u32[]{:S(2)}, u32[]{:S(2)}) %all-to-all-start) | async-done | bytes 80128 | tf_op jit(solution)/shard_map/all_to_all | solution.py:98
  36.1 44.8 %all-gather.4.cloned.1.call-done = bf16[1024,2730]{1,0:T(8,128)(2,1)} async-done(((bf16[32,2730]{1,0:T(8,128)(2,1)}), bf16[1024,2730]{1,0:T(8,128)(2,1)}) %all-gather.4.cloned.1.call-update) | async-done | bytes 5591056 | tf_op jit(solution)/shard_map/all_gather | solution.py:67
  80.9 5.2 fusion.16
  86.1 63.7 %all-gather.6.cloned.1.call-done = bf16[1024,2730]{1,0:T(8,128)(2,1)} async-done(((bf16[32,2730]{1,0:T(8,128)(2,1)}), bf16[1024,2730]{1,0:T(8,128)(2,1)}) %all-gather.6.cloned.1.call-update) | async-done | bytes 5591056 | tf_op jit(solution)/shard_map/all_gather | solution.py:68
  149.8 68.9 %all-gather.8.cloned.1.call-done = bf16[2730,1024]{0,1:T(8,128)(2,1)} async-done(((bf16[2730,32]{0,1:T(8,128)(2,1)}), bf16[2730,1024]{0,1:T(8,128)(2,1)}) %all-gather.8.cloned.1.call-update) | async-done | bytes 5591056 | tf_op jit(solution)/shard_map/all_gather | solution.py:73
  218.7 7.9 %fusion.72 = (f32[176]{0:T(256)S(1)}, f32[176,1024]{1,0:T(8,128)S(1)}) fusion(bf16[2730,1024]{0,1:T(8,128)(2,1)} %all-gather.8.cloned.1.call-done, bf16[1024,2730]{1,0:T(8,128)(2,1)} %all-gather.6.cloned.1.call-done, f32[176,2730]{1,0:T(8,128)} %fusion.16, bf16[176,1024]{1,0:T(8,128)(2,1)S(1)} %copy-done.2, f32[1024]{0:T(1024)S(1)} %copy-done.11, ...), kind=kOutput, calls=%fused_computation.126 | convolution fusion | flops 1972370688 | bytes 14191552 | tf_op jit(solution)/shard_map/dot_general | solution.py:74
  228.1 116.9 %gather_fusion = bf16[20024]{0:T(1024)(128)(2,1)S(1)} fusion(bf16[11264]{0:T(1024)(128)(2,1)S(1)} %reshape.331, s32[20480]{0:T(1024)S(1)} %pad_clamp_fusion), kind=kCustom, calls=%fused_computation | custom fusion | bytes 160192 | tf_op jit(solution)/shard_map/gather | solution.py:90
  345.9 3.9 all-to-all-start.2
  350.1 31.8 %all_gather.15 = bf16[1408,128]{1,0:T(8,128)(2,1)S(1)} all-gather(bf16[176,128]{1,0:T(8,128)(2,1)S(1)} %convolution_convert_fusion), channel_id=1, replica_groups=mesh['cam'=4,'tile'=8] {'tile'}, dimensions={0}, use_global_device_ids=true | all-gather | bytes 405504 | tf_op jit(solution)/shard_map/all_gather | solution.py:87
  382.2 140.2 %while.11 = (s32[]{:T(128)}, f32[2048,128]{1,0:T(8,128)S(1)}, s32[2,10012]{1,0:T(2,128)S(1)}, s32[2,10012]{1,0:T(2,128)S(1)}, f32[2,10012]{1,0:T(2,128)S(1)}, /*...) while((s32[]{:T(128)}, f32[2048,128]{1,0:T(8,128)S(1)}, ...), condition=%wide.region_8.9_spmd.clone, body=%wide.region_6.8_spmd.clone.sunk | while | flops 2215176960 | bytes 25546404 | solution.py:124
  382.5 57.1 %scatter_custom_fusion.6 = f32[1441792]{0:T(1024)} fusion(s32[10012]{0:T(1024)S(1)} %fusion.109, f32[10012]{0:T(1024)S(1)} %dynamic-slice_reduce_fusion.2, f32[]{:T(128)} %constant.24.clone.3..sunk), kind=kCustom, calls=%fused_computation.2.clone.1 | custom fusion | flops 10012 | bytes 5767172 | tf_op jit(solution)/shard_map/while/body/eval_jaxpr/scatter-add | solution.py:117
  439.6 7.6 %reshape.390 = f32[2048,704]{1,0:T(8,128)} reshape(f32[1441792]{0:T(1024)} %scatter_custom_fusion.6) | data formatting | bytes 11534336 | tf_op jit(solution)/shard_map/while/body/eval_jaxpr/reshape | solution.py:118
  447.2 5.1 convolution_add_fusion.18
  452.6 57.1 %scatter_custom_fusion.6 = f32[1441792]{0:T(1024)} fusion(s32[10012]{0:T(1024)S(1)} %fusion.109, f32[10012]{0:T(1024)S(1)} %dynamic-slice_reduce_fusion.2, f32[]{:T(128)} %constant.24.clone.3..sunk), kind=kCustom, calls=%fused_computation.2.clone.1 | custom fusion | flops 10012 | bytes 5767172 | tf_op jit(solution)/shard_map/while/body/eval_jaxpr/scatter-add | solution.py:117
  509.8 7.6 %reshape.390 = f32[2048,704]{1,0:T(8,128)} reshape(f32[1441792]{0:T(1024)} %scatter_custom_fusion.6) | data formatting | bytes 11534336 | tf_op jit(solution)/shard_map/while/body/eval_jaxpr/reshape | solution.py:118
  517.4 5.1 convolution_add_fusion.18
  522.5 3.4 collective-permute-start
  527.3 2.5 collective-permute-done
  529.9 4.4 collective-permute-done.1
  534.4 1.3 pad_slice_fusion.1
  (93 shorter events, 20.1 us)
Async XLA Ops:
  6.5 343.3 %copy-start = (bf16[1024,128]{1,0:T(8,128)(2,1)S(1)}, bf16[1024,128]{1,0:T(8,128)(2,1)}, u32[]{:S(2)}) copy-start(bf16[1024,128]{1,0:T(8,128)(2,1)} %param.24) | copy-start | bytes 786436
  6.5 14.7 %copy-start.2 = (bf16[176,1024]{1,0:T(8,128)(2,1)S(1)}, bf16[176,1024]{1,0:T(8,128)(2,1)}, u32[]{:S(2)}) copy-start(bf16[176,1024]{1,0:T(8,128)(2,1)} %param.17) | copy-start | bytes 1081348
  6.5 14.0 %copy-start.6 = (s32[1,8,2503]{2,1,0:T(8,128)S(1)}, s32[1,8,2503]{2,1,0:T(8,128)}, u32[]{:S(2)}) copy-start(s32[1,8,2503]{2,1,0:T(8,128)} %param.26) | copy-start | bytes 240292
  6.5 74.3 %all-gather.4.cloned.1.call-start = ((), (), s32[]{:S(2)}) async-start(), calls=%async_computation.3 | async-start | bytes 5947392 | tf_op jit(solution)/shard_map/all_gather | solution.py:67
  7.3 73.6 %copy-start.11 = (f32[1024]{0:T(1024)S(1)}, f32[1024]{0:T(1024)}, u32[]{:S(2)}) copy-start(f32[1024]{0:T(1024)} %param.18) | copy-start | bytes 12292
  7.3 142.5 %all-gather.6.cloned.1.call-start = ((), (), s32[]{:S(2)}) async-start(), calls=%async_computation.4 | async-start | bytes 5947392 | tf_op jit(solution)/shard_map/all_gather | solution.py:68
  8.0 210.7 %all-gather.8.cloned.1.call-start = ((), (), s32[]{:S(2)}) async-start(), calls=%async_computation.5 | async-start | bytes 5947392 | tf_op jit(solution)/shard_map/all_gather | solution.py:73
  10.6 14.4 %all-to-all-start.1 = ((s32[8,1,2503]{2,1,0:T(1,128)}), s32[8,1,2503]{2,1,0:T(1,128)S(1)}, u32[]{:S(2)}, u32[]{:S(2)}) async-start(s32[8,1,2503]{2,1,0:T(1,128)} %and_select_fusion), calls=%async_computation.1 | async-start | bytes 163840 | tf_op jit(solution)/shard_map/all_to_all | solution.py:97
  25.0 10.6 %all-to-all-start = ((s32[8,1,2503]{2,1,0:T(1,128)}), s32[8,1,2503]{2,1,0:T(1,128)S(1)}, u32[]{:S(2)}, u32[]{:S(2)}) async-start(s32[8,1,2503]{2,1,0:T(1,128)} %all_to_all.14), calls=%async_computation | async-start | bytes 163840 | tf_op jit(solution)/shard_map/all_to_all | solution.py:98
  86.1 140.7 %copy-start.7 = (f32[1024]{0:T(1024)S(1)}, f32[1024]{0:T(1024)}, u32[]{:S(2)}) copy-start(f32[1024]{0:T(1024)} %param.22) | copy-start | bytes 12292
  226.6 0.9 copy-start.5
  228.1 117.0 %copy-start.8 = (s32[1,8]{1,0:T(1,128)S(1)}, s32[1,8]{1,0:T(1,128)}, u32[]{:S(2)}) copy-start(s32[1,8]{1,0:T(1,128)} %param.27) | copy-start | bytes 100
  345.9 36.0 %all-to-all-start.2 = ((bf16[8,1,2503]{2,1,0:T(2,128)(2,1)}), bf16[8,1,2503]{2,1,0:T(2,128)(2,1)S(1)}, u32[]{:S(2)}, u32[]{:S(2)}) async-start(bf16[8,1,2503]{2,1,0:T(2,128)(2,1)} %fusion.27), calls=%async_computation.2 | async-start | bytes 163840 | tf_op jit(solution)/shard_map/all_to_all | solution.py:93
  522.5 7.3 %collective-permute-start = (bf16[2,2,256,128]{3,2,1,0:T(8,128)(2,1)S(1)}, bf16[2,2,256,128]{3,2,1,0:T(8,128)(2,1)S(1)}, u32[]{:S(2)}, u32[]{:S(2)}) collective-permute-start(bf16[2,2,256,128]{3,2,1,0:T(8,128)(2,1)S(1)} %get-tuple-element.89), channel_id=1, source_target_pairs={{0,1},{1,2},{2,3},{3,4},{4,5},{5,6},{6,7},{8,9},{9,10},{10,11},{11... | collective-permute-start | bytes 786440 | tf_op jit(solution)/shard_map/ppermute | solution.py:18
  526.0 8.3 %collective-permute-start.1 = (bf16[2,2,256,128]{3,2,1,0:T(8,128)(2,1)S(1)}, bf16[2,2,256,128]{3,2,1,0:T(8,128)(2,1)S(1)}, u32[]{:S(2)}, u32[]{:S(2)}) collective-permute-start(bf16[2,2,256,128]{3,2,1,0:T(8,128)(2,1)S(1)} %get-tuple-element.90), channel_id=1, source_target_pairs={{1,0},{2,1},{3,2},{4,3},{5,4},{6,5},{7,6},{9,8},{10,9},{11,10},{12... | collective-permute-start | bytes 786440 | tf_op jit(solution)/shard_map/ppermute | solution.py:19
  534.4 1.3 copy-start.3
  538.7 0.7 copy-start.10
  539.6 1.0 copy-start.4
  542.9 0.7 copy-start.9
  542.9 1.6 copy-start.1
Sparse Core Ops, SparseCore 0:
  10.2 70.5 all-gather.3
  83.8 65.9 all-gather.5
  152.7 65.9 all-gather.7
where the time goes:
time: 552 us; the launch traced here: 551 us
  waiting for transfers between devices  197 us (36%)
  local copies, waits for them, and re-layouts  138 us (25%)
  other arithmetic  122 us (22%)
  blocking collectives  31.8 us (6%)
  matrix products  29.4 us (5%)
  starting transfers between devices  19.4 us (4%)
  between operations  13.6 us (2%)
    gather x2, local copies, waits for them, and re-layouts, on_device(): depth.reshape(-1)[own_points.reshape(-1)]  117 us
    scatter-add x2, other arithmetic, splat_step(): spread_flat.at[cell_row * batch_tokens + token_row].add(weight_row)  114 us
    all_gather x1, waiting for transfers between devices, on_device(): lax.all_gather(down_weight, ('cam', 'tile'), axis=1, tiled=True)  68.9 us
    all_gather x1, waiting for transfers between devices, on_device(): lax.all_gather(up_weight, ('cam', 'tile'), axis=0, tiled=True)  63.7 us
    all_gather x1, waiting for transfers between devices, on_device(): lax.all_gather(gate_weight, ('cam', 'tile'), axis=0, tiled=True)  44.8 us
    all_gather x1, blocking collectives, on_device(): context_all = lax.all_gather(context, 'tile', axis=0, tiled=True)  31.8 us
    reshape x2, local copies, waits for them, and re-layouts, splat_step(): spread_table = spread_flat.reshape(cell_count, batch_tokens)  15.2 us
  transfers between devices with their start and end apart: 8, of which 7 were waited for; matrix products, arithmetic and copies ran while one was open for 2% of the time, Pallas kernels for 0%

commit v1 on v0

v1 whole, which is shorter than its diff:
```python
import jax
import jax.numpy as jnp
from jax import lax
from jax.experimental import pallas as pl
from jax.experimental.pallas import tpu as pltpu
from jax.sharding import PartitionSpec as P

ROWS_DEV = 4
GRID_W = 256
SCN = 2


def extended_2(value, sides, width):
    for axis, dim in sides:
        size, length = (lax.axis_size(axis), value.shape[dim])
        up = [(i, (i + 1) % size) for i in range(size - 1)]
        down = [(j, i) for i, j in up]
        last = lax.slice_in_dim(value, length - width, length, axis=dim)
        leading = lax.slice_in_dim(value, 0, width, axis=dim)
        before = lax.ppermute(last, axis, up)
        after = lax.ppermute(leading, axis, down)
        value = jnp.concatenate([before, value, after], axis=dim)
    return value


def layer_norm(values, gain):
    center = values - jnp.mean(values, axis=-1, keepdims=True)
    spread = jnp.mean(center * center, axis=-1, keepdims=True)
    return center * lax.rsqrt(spread + 1e-06) * gain


def conv_rows(extended, weight):
    scenes = extended.shape[0]
    out_rows = extended.shape[1] - 2
    columns = extended.shape[2]
    padded = jnp.pad(extended, ((0, 0), (0, 0), (1, 1), (0, 0)))
    total = jnp.zeros((scenes * out_rows * columns, weight.shape[3]), jnp.float32)
    for row_shift in range(3):
        for col_shift in range(3):
            window = padded[:, row_shift : row_shift + out_rows, col_shift : col_shift + columns, :]
            window = window.reshape(-1, weight.shape[2])
            total = total + jnp.dot(
                window, weight[row_shift, col_shift], preferred_element_type=jnp.float32
            )
    return total.reshape(scenes, out_rows, columns, weight.shape[3])


CHUNK = 512


def splat_kernel(rows_ref, table_ref, out_ref):
    sources, _, slots = rows_ref.shape
    tokens = table_ref.shape[2]
    half, wide = out_ref.shape
    channels = wide // 2
    bins = table_ref.shape[1] - channels
    chunks = slots // CHUNK
    out_ref[...] = jnp.zeros_like(out_ref)

    def step(i, carry):
        source = i // chunks
        start = pl.multiple_of((i % chunks) * CHUNK, CHUNK)
        rows = rows_ref[source, :, pl.ds(start, CHUNK)]
        token, depth_bin, cell = rows[0:1], rows[1:2], rows[2:3]
        token_ids = lax.broadcasted_iota(jnp.int32, (tokens, CHUNK), 0)
        pick = jnp.where(token_ids == token, 1.0, 0.0).astype(jnp.bfloat16)
        got = jnp.dot(table_ref[source], pick, preferred_element_type=jnp.float32)
        bin_ids = lax.broadcasted_iota(jnp.int32, (bins, CHUNK), 0)
        weight = jnp.sum(
            jnp.where(bin_ids == depth_bin, got[:bins], 0.0), axis=0, keepdims=True
        )
        upper = cell >= half
        low = jnp.where(upper, 0.0, weight) * got[bins:]
        high = jnp.where(upper, weight, 0.0) * got[bins:]
        lifted = jnp.concatenate([low, high], axis=0).astype(jnp.bfloat16)
        local = jnp.where(upper, cell - half, cell)
        cell_ids = lax.broadcasted_iota(jnp.int32, (half, CHUNK), 0)
        place = jnp.where(cell_ids == local, 1.0, 0.0).astype(jnp.bfloat16)
        out_ref[...] += lax.dot_general(
            place, lifted, (((1,), (1,)), ((), ())), preferred_element_type=jnp.float32
        )
        return carry

    lax.fori_loop(0, sources * chunks, step, 0)


def splat_cells(rows, table, cell_count, channels):
    half = cell_count // 2
    out = pl.pallas_call(
        splat_kernel,
        out_shape=jax.ShapeDtypeStruct((half, 2 * channels), jnp.float32),
        in_specs=[pl.BlockSpec(memory_space=pltpu.VMEM)] * 2,
        out_specs=pl.BlockSpec(memory_space=pltpu.VMEM),
        compiler_params=pltpu.CompilerParams(vmem_limit_bytes=48 * 1024 * 1024),
        cost_estimate=pl.CostEstimate(
            flops=2 * cell_count * channels * rows.shape[0] * rows.shape[2],
            bytes_accessed=4 * cell_count * channels,
            transcendentals=0,
        ),
    )(rows, table)
    return jnp.concatenate([out[:, :channels], out[:, channels:]], axis=0)


def slot_rows(slot_point, slot_cell, slot_count, points, bins_count):
    tiles, slots = slot_point.shape[1:]
    live = jnp.arange(slots, dtype=jnp.int32)[None, :] < slot_count.reshape(tiles, 1)
    packed = jnp.where(live, slot_point.reshape(tiles, slots), points) * 65536
    packed = packed + slot_cell.reshape(tiles, slots)
    got = lax.all_to_all(packed, "tile", split_axis=0, concat_axis=0, tiled=True)
    got = jnp.pad(got, ((0, 0), (0, -slots % CHUNK)), constant_values=points * 65536)
    point = got // 65536
    zero = jnp.zeros_like(got)
    parts = [point // bins_count, point % bins_count, got % 65536]
    return jnp.stack(parts + [zero] * 5, axis=1)


def on_device(
    tokens,
    ln_gain,
    gate_weight,
    up_weight,
    down_weight,
    head_gain,
    depth_weight,
    context_weight,
    slot_point,
    slot_cell,
    slot_count,
    conv1_weight,
    conv1_bias,
    conv2_weight,
    conv2_bias,
):
    tiles = lax.axis_size("tile")
    token_count = tokens.shape[0]
    bins_count = depth_weight.shape[1]
    rows = slot_rows(slot_point, slot_cell, slot_count, token_count * bins_count, bins_count)
    inputs = tokens.astype(jnp.float32)
    normed = layer_norm(inputs, ln_gain).astype(jnp.bfloat16)
    gate_whole, up_whole = (
        lax.all_gather(gate_weight, ("cam", "tile"), axis=0, tiled=True),
        lax.all_gather(up_weight, ("cam", "tile"), axis=0, tiled=True),
    )
    gate_full = jnp.dot(normed, gate_whole, preferred_element_type=jnp.float32)
    up_full = jnp.dot(normed, up_whole, preferred_element_type=jnp.float32)
    hidden = (jax.nn.silu(gate_full) * up_full).astype(jnp.bfloat16)
    down_whole = lax.all_gather(down_weight.T, ("cam", "tile"), axis=0, tiled=True)
    branch_out = lax.dot_general(
        hidden, down_whole, (((1,), (1,)), ((), ())), preferred_element_type=jnp.float32
    )
    updated = inputs + branch_out
    head_input = layer_norm(updated, head_gain).astype(jnp.bfloat16)
    contract = (((0,), (1,)), ((), ()))
    logits = lax.dot_general(
        depth_weight, head_input, contract, preferred_element_type=jnp.float32
    )
    context = lax.dot_general(
        context_weight, head_input, contract, preferred_element_type=jnp.float32
    )
    depth = jax.nn.softmax(logits, axis=0)
    channels = context.shape[0]
    table = jnp.concatenate([depth, context], axis=0).astype(jnp.bfloat16)
    table_all = lax.all_gather(table, "tile", axis=0, tiled=False)
    cell_count = SCN * ROWS_DEV * GRID_W
    splat = splat_cells(rows, table_all, cell_count, channels)
    bev = splat.astype(jnp.bfloat16).reshape(SCN, ROWS_DEV, GRID_W, channels)
    extended = extended_2(bev, (("tile", 1),), 2)
    middle_wide = jnp.maximum(conv_rows(extended, conv1_weight) + conv1_bias, 0.0)
    global_rows = lax.axis_index("tile") * ROWS_DEV - 1 + jnp.arange(ROWS_DEV + 2, dtype=jnp.int32)
    inside = (global_rows >= 0) & (global_rows < tiles * ROWS_DEV)
    middle_ext = jnp.where(inside[None, :, None, None], middle_wide, 0.0).astype(jnp.bfloat16)
    result = bev.astype(jnp.float32) + conv_rows(middle_ext, conv2_weight) + conv2_bias
    return result.astype(jnp.bfloat16)


def solution(mesh):
    return jax.shard_map(
        on_device,
        mesh=mesh,
        in_specs=(
            P(("cam", "tile"), None),
            P(),
            P(("cam", "tile"), None),
            P(("cam", "tile"), None),
            P(None, ("cam", "tile")),
            P(),
            P(),
            P(),
            P(("cam", "tile"), None, None),
            P(("cam", "tile"), None, None),
            P(("cam", "tile"), None),
            P(),
            P(),
            P(),
            P(),
        ),
        out_specs=P("cam", "tile", None, None),
        check_vma=False,
    )
```

time: 552 us -> 315 us (0.57)
  local copies, waits for them, and re-layouts: 138 us -> 5.32 us
  other arithmetic: 122 us -> 6.38 us
  Pallas kernels: 0 us -> 27.4 us
  matrix products: 29.4 us -> 19.3 us
  starting transfers between devices: 19.4 us -> 10.8 us
    gather x2 -> x0, local copies, waits for them, and re-layouts: 117 us -> none  [on_device(): depth.reshape(-1)[own_points.reshape(-1)]]
    scatter-add x2 -> x0, other arithmetic: 114 us -> none  [splat_step(): spread_flat.at[cell_row * batch_tokens + token_row].add(weight_row)]
    pallas_call x0 -> x1, Pallas kernels: none -> 27.4 us  [splat_cells(): pl.pallas_call(splat_kernel, out_shape=jax.ShapeDtypeStruct((half, 2 * ch...]
    reshape x5 -> x0, local copies, waits for them, and re-layouts: 15.6 us -> none  [the longest x2 15.2 us: splat_step(): spread_table = spread_flat.reshape(cell_count, batch_tokens)]
    dot_general x5 -> x3, matrix products: 18.5 us -> 8.39 us  [the longest x1 7.89 us: on_device(): lax.dot_general(hidden, down_whole, (((1,), (1,)), ((), ())), preferred_e...]
    all_gather x1, waiting for transfers between devices: 44.8 us -> 53.8 us  [on_device(): lax.all_gather(gate_weight, ('cam', 'tile'), axis=0, tiled=True)]
    all_to_all x3 -> x1, starting transfers between devices: 14.6 us -> 7.28 us  [slot_rows(): lax.all_to_all(packed, 'tile', split_axis=0, concat_axis=0, tiled=True)]
    all_to_all x3 -> x1, waiting for transfers between devices: 10.4 us -> 4.69 us  [slot_rows(): lax.all_to_all(packed, 'tile', split_axis=0, concat_axis=0, tiled=True)]
  transfers between devices with their start and end apart: 8 -> 6, of which waited for: 7 -> 6; matrix products, arithmetic and copies ran while one was open for 2% -> 3% of each run, Pallas kernels for 0% -> 0%
where the time goes in v1:
time: 315 us
  waiting for transfers between devices  200 us (63%)
  blocking collectives  31.9 us (10%)
  Pallas kernels  27.4 us (9%)
  matrix products  19.3 us (6%)
  between operations  13.5 us (4%)
  starting transfers between devices  10.8 us (3%)
  other arithmetic  6.38 us (2%)
  local copies, waits for them, and re-layouts  5.32 us (2%)
    all_gather x1, waiting for transfers between devices, on_device(): lax.all_gather(down_weight.T, ('cam', 'tile'), axis=0, tiled=True)  68.9 us
    all_gather x1, waiting for transfers between devices, on_device(): lax.all_gather(up_weight, ('cam', 'tile'), axis=0, tiled=True)  63.7 us
    all_gather x1, waiting for transfers between devices, on_device(): lax.all_gather(gate_weight, ('cam', 'tile'), axis=0, tiled=True)  53.8 us
    all_gather x1, blocking collectives, on_device(): table_all = lax.all_gather(table, 'tile', axis=0, tiled=False)  31.9 us
    pallas_call x1, Pallas kernels, splat_cells(): pl.pallas_call(splat_kernel, out_shape=jax.ShapeDtypeStruct((half, 2 * ch...  27.4 us
    dot_general x1, matrix products, on_device(): lax.dot_general(hidden, down_whole, (((1,), (1,)), ((), ())), preferred_e...  7.89 us
    all_to_all x1, starting transfers between devices, slot_rows(): lax.all_to_all(packed, 'tile', split_axis=0, concat_axis=0, tiled=True)  7.28 us
  transfers between devices with their start and end apart: 6, of which 6 were waited for; matrix products, arithmetic and copies ran while one was open for 3% of the time, Pallas kernels for 0%

profile of v1, /device:TPU:0, one launch (start us, length us, event | category | flops | bytes accessed | tf_op | source)
XLA Modules:
  0.0 314.5 jit_solution(14556880500038234669)
XLA Ops:
  6.5 0.7 all-gather.4.cloned.1.call-update
  7.3 0.7 all-gather.6.cloned.1.call-update
  8.1 0.7 all-gather.8.cloned.1.call-update
  8.7 1.7 fusion.25
  10.5 7.3 %all-to-all-start = ((s32[8,1,2503]{2,1,0:T(1,128)}), s32[8,1,2503]{2,1,0:T(1,128)S(1)}, u32[]{:S(2)}, u32[]{:S(2)}) async-start(s32[8,1,2503]{2,1,0:T(1,128)} %fusion.25), calls=%async_computation | async-start | bytes 163840 | tf_op jit(solution)/shard_map/all_to_all | solution.py:109
  17.8 1.1 convert_reduce_fusion
  18.9 1.3 fusion.6
  20.2 4.7 %all-to-all-done = s32[8,1,2503]{2,1,0:T(1,128)S(1)} async-done(((s32[8,1,2503]{2,1,0:T(1,128)}), s32[8,1,2503]{2,1,0:T(1,128)S(1)}, u32[]{:S(2)}, u32[]{:S(2)}) %all-to-all-start) | async-done | bytes 80128 | tf_op jit(solution)/shard_map/all_to_all | solution.py:109
  25.4 1.1 stack.19.rows_ref
  26.5 53.8 %all-gather.4.cloned.1.call-done = bf16[1024,2730]{1,0:T(8,128)(2,1)} async-done(((bf16[32,2730]{1,0:T(8,128)(2,1)}), bf16[1024,2730]{1,0:T(8,128)(2,1)}) %all-gather.4.cloned.1.call-update) | async-done | bytes 5591056 | tf_op jit(solution)/shard_map/all_gather | solution.py:141
  80.3 5.2 %fusion.11 = f32[176,2730]{1,0:T(8,128)} fusion(bf16[1024,2730]{1,0:T(8,128)(2,1)} %all-gather.4.cloned.1.call-done, bf16[176,1024]{1,0:T(8,128)(2,1)S(1)} %copy-done.2, f32[1024]{0:T(1024)S(1)} %copy-done.9, f32[176]{0:T(256)S(1)} %add_rsqrt_fusion.1, f32[176]{0:T(256)S(1)} %broadcast_multiply_fusion.1), kind=kOutput, calls=%fused_computation.43 | convolution fusion | flops 984924160 | bytes 7878912 | tf_op jit(solution)/shard_map/dot_general | solution.py:144
  85.6 63.7 %all-gather.6.cloned.1.call-done = bf16[1024,2730]{1,0:T(8,128)(2,1)} async-done(((bf16[32,2730]{1,0:T(8,128)(2,1)}), bf16[1024,2730]{1,0:T(8,128)(2,1)}) %all-gather.6.cloned.1.call-update) | async-done | bytes 5591056 | tf_op jit(solution)/shard_map/all_gather | solution.py:142
  149.2 68.9 %all-gather.8.cloned.1.call-done = bf16[1024,2730]{1,0:T(8,128)(2,1)} async-done(((bf16[32,2730]{1,0:T(8,128)(2,1)}), bf16[1024,2730]{1,0:T(8,128)(2,1)}) %all-gather.8.cloned.1.call-update) | async-done | bytes 5591056 | tf_op jit(solution)/shard_map/all_gather | solution.py:147
  218.2 7.9 %fusion.74 = (f32[176]{0:T(256)S(1)}, f32[176,1024]{1,0:T(8,128)S(1)}) fusion(bf16[1024,2730]{1,0:T(8,128)(2,1)} %all-gather.8.cloned.1.call-done, bf16[1024,2730]{1,0:T(8,128)(2,1)} %all-gather.6.cloned.1.call-done, f32[176,2730]{1,0:T(8,128)} %fusion.11, bf16[176,1024]{1,0:T(8,128)(2,1)S(1)} %copy-done.2, f32[1024]{0:T(1024)S(1)} %copy-done.9, ...), kind=kOutput, calls=%fused_computation.131 | convolution fusion | flops 1972370688 | bytes 14191552 | tf_op jit(solution)/shard_map/dot_general | solution.py:148
  226.5 0.5 copy-done.5
  227.8 31.9 %all_gather.16 = bf16[8,192,176]{1,2,0:T(8,128)(2,1)S(1)} all-gather(bf16[1,192,176]{1,2,0:T(8,128)(2,1)S(1)} %pad_maximum_fusion.4), channel_id=1, replica_groups=mesh['cam'=4,'tile'=8] {'tile'}, dimensions={0}, use_global_device_ids=true | all-gather | bytes 608256 | tf_op jit(solution)/shard_map/all_gather | solution.py:163
  260.0 27.4 %shard_map.145 = f32[1024,256]{1,0:T(8,128)S(1)} custom-call(s32[8,8,2560]{2,1,0:T(8,128)S(1)} %stack.19.rows_ref, bf16[8,192,176]{2,1,0:T(8,128)(2,1)S(1)} %copy.22.table_ref), custom_call_target="tpu_custom_call" | custom-call | flops 10737418240 | bytes 1048576 | tf_op jit(solution)/shard_map/pallas_call | solution.py:89
  287.5 1.9 collective-permute-start
  289.5 1.5 collective-permute-start.1
  291.0 2.4 collective-permute-done
  293.3 4.4 %collective-permute-done.1 = bf16[2,2,256,128]{3,2,1,0:T(8,128)(2,1)S(1)} collective-permute-done((bf16[2,2,256,128]{3,2,1,0:T(8,128)(2,1)S(1)}, bf16[2,2,256,128]{3,2,1,0:T(8,128)(2,1)S(1)}, u32[]{:S(2)}, u32[]{:S(2)}) %collective-permute-start.1) | collective-permute-done | bytes 262176 | tf_op jit(solution)/shard_map/ppermute | solution.py:21
  297.9 1.3 pad_slice_fusion.1
  303.1 1.0 pad_slice_fusion.6
  307.0 0.9 add_convert_fusion
  (68 shorter events, 9.1 us)
Async XLA Ops:
  6.5 220.9 %copy-start = (bf16[1024,128]{1,0:T(8,128)(2,1)S(1)}, bf16[1024,128]{1,0:T(8,128)(2,1)}, u32[]{:S(2)}) copy-start(bf16[1024,128]{1,0:T(8,128)(2,1)} %param.22) | copy-start | bytes 786436
  6.5 73.8 %all-gather.4.cloned.1.call-start = ((), (), s32[]{:S(2)}) async-start(), calls=%async_computation.1 | async-start | bytes 5947392 | tf_op jit(solution)/shard_map/all_gather | solution.py:141
  7.3 142.0 %all-gather.6.cloned.1.call-start = ((), (), s32[]{:S(2)}) async-start(), calls=%async_computation.2 | async-start | bytes 5947392 | tf_op jit(solution)/shard_map/all_gather | solution.py:142
  8.0 210.2 %all-gather.8.cloned.1.call-start = ((), (), s32[]{:S(2)}) async-start(), calls=%async_computation.3 | async-start | bytes 5947392 | tf_op jit(solution)/shard_map/all_gather | solution.py:147
  10.5 14.4 %all-to-all-start = ((s32[8,1,2503]{2,1,0:T(1,128)}), s32[8,1,2503]{2,1,0:T(1,128)S(1)}, u32[]{:S(2)}, u32[]{:S(2)}) async-start(s32[8,1,2503]{2,1,0:T(1,128)} %fusion.25), calls=%async_computation | async-start | bytes 163840 | tf_op jit(solution)/shard_map/all_to_all | solution.py:109
  18.9 61.5 %copy-start.2 = (bf16[176,1024]{1,0:T(8,128)(2,1)S(1)}, bf16[176,1024]{1,0:T(8,128)(2,1)}, u32[]{:S(2)}) copy-start(bf16[176,1024]{1,0:T(8,128)(2,1)} %param.15) | copy-start | bytes 1081348
  18.9 61.5 %copy-start.9 = (f32[1024]{0:T(1024)S(1)}, f32[1024]{0:T(1024)}, u32[]{:S(2)}) copy-start(f32[1024]{0:T(1024)} %param.16) | copy-start | bytes 12292
  85.6 140.7 %copy-start.6 = (f32[1024]{0:T(1024)S(1)}, f32[1024]{0:T(1024)}, u32[]{:S(2)}) copy-start(f32[1024]{0:T(1024)} %param.20) | copy-start | bytes 12292
  226.0 0.9 copy-start.5
  287.5 5.8 %collective-permute-start = (bf16[2,2,256,128]{3,2,1,0:T(8,128)(2,1)S(1)}, bf16[2,2,256,128]{3,2,1,0:T(8,128)(2,1)S(1)}, u32[]{:S(2)}, u32[]{:S(2)}) collective-permute-start(bf16[2,2,256,128]{3,2,1,0:T(8,128)(2,1)S(1)} %get-tuple-element.23), channel_id=1, source_target_pairs={{0,1},{1,2},{2,3},{3,4},{4,5},{5,6},{6,7},{8,9},{9,10},{10,11},{11... | collective-permute-start | bytes 786440 | tf_op jit(solution)/shard_map/ppermute | solution.py:20
  289.5 8.3 %collective-permute-start.1 = (bf16[2,2,256,128]{3,2,1,0:T(8,128)(2,1)S(1)}, bf16[2,2,256,128]{3,2,1,0:T(8,128)(2,1)S(1)}, u32[]{:S(2)}, u32[]{:S(2)}) collective-permute-start(bf16[2,2,256,128]{3,2,1,0:T(8,128)(2,1)S(1)} %get-tuple-element.24), channel_id=1, source_target_pairs={{1,0},{2,1},{3,2},{4,3},{5,4},{6,5},{7,6},{9,8},{10,9},{11,10},{12... | collective-permute-start | bytes 786440 | tf_op jit(solution)/shard_map/ppermute | solution.py:21
  297.9 1.3 copy-start.3
  302.2 0.7 copy-start.8
  303.1 1.0 copy-start.4
  306.4 0.7 copy-start.7
  306.4 1.6 copy-start.1
Sparse Core Ops, SparseCore 0:
  10.2 70.0 all-gather.3
  83.2 65.9 all-gather.5
  152.2 65.9 all-gather.7

commit v2 on v1

--- a/solution.py
+++ b/solution.py
@@ -48,52 +48,102 @@
 CHUNK = 512
 
 
-def splat_kernel(rows_ref, table_ref, out_ref):
-    sources, _, slots = rows_ref.shape
-    tokens = table_ref.shape[2]
+def splat_kernel(rows_ref, table_ref, out_ref, held, send_sem, recv_sem):
+    tiles, _, slots = rows_ref.shape
+    tokens = table_ref.shape[1]
     half, wide = out_ref.shape
     channels = wide // 2
-    bins = table_ref.shape[1] - channels
+    bins = table_ref.shape[0] - channels
     chunks = slots // CHUNK
-    out_ref[...] = jnp.zeros_like(out_ref)
-
-    def step(i, carry):
-        source = i // chunks
-        start = pl.multiple_of((i % chunks) * CHUNK, CHUNK)
-        rows = rows_ref[source, :, pl.ds(start, CHUNK)]
-        token, depth_bin, cell = rows[0:1], rows[1:2], rows[2:3]
-        token_ids = lax.broadcasted_iota(jnp.int32, (tokens, CHUNK), 0)
-        pick = jnp.where(token_ids == token, 1.0, 0.0).astype(jnp.bfloat16)
-        got = jnp.dot(table_ref[source], pick, preferred_element_type=jnp.float32)
-        bin_ids = lax.broadcasted_iota(jnp.int32, (bins, CHUNK), 0)
-        weight = jnp.sum(
-            jnp.where(bin_ids == depth_bin, got[:bins], 0.0), axis=0, keepdims=True
+    me = lax.axis_index("tile")
+
+    def table_copy(k):
+        return pltpu.make_async_remote_copy(
+            src_ref=table_ref,
+            dst_ref=held.at[k],
+            send_sem=send_sem.at[k],
+            recv_sem=recv_sem.at[k],
+            device_id={"tile": lax.rem(me - k + tiles, tiles)},
+            device_id_type=pl.DeviceIdType.MESH,
         )
-        upper = cell >= half
-        low = jnp.where(upper, 0.0, weight) * got[bins:]
-        high = jnp.where(upper, weight, 0.0) * got[bins:]
-        lifted = jnp.concatenate([low, high], axis=0).astype(jnp.bfloat16)
-        local = jnp.where(upper, cell - half, cell)
-        cell_ids = lax.broadcasted_iota(jnp.int32, (half, CHUNK), 0)
-        place = jnp.where(cell_ids == local, 1.0, 0.0).astype(jnp.bfloat16)
-        out_ref[...] += lax.dot_general(
-            place, lifted, (((1,), (1,)), ((), ())), preferred_element_type=jnp.float32
+
+    barrier = pltpu.get_barrier_semaphore()
+
+    def greet(k, carry):
+        other = lax.rem(me + k, tiles)
+        pl.semaphore_signal(
+            barrier, inc=1, device_id={"tile": other}, device_id_type=pl.DeviceIdType.MESH
         )
         return carry
 
-    lax.fori_loop(0, sources * chunks, step, 0)
+    def send(k, carry):
+        table_copy(k).start()
+        return carry
+
+    def finish(k, carry):
+        table_copy(k).wait_send()
+        return carry
+
+    lax.fori_loop(1, tiles, greet, 0)
+    pl.semaphore_wait(barrier, tiles - 1)
+    lax.fori_loop(1, tiles, send, 0)
+    out_ref[...] = jnp.zeros_like(out_ref)
+    held[0] = table_ref[...]
+
+    def one_source(k, carry):
+        @pl.when(k > 0)
+        def _():
+            table_copy(k).wait_recv()
+
+        source = lax.rem(me + k, tiles)
+
+        def step(i, inner):
+            start = pl.multiple_of(i * CHUNK, CHUNK)
+            rows = rows_ref[source, :, pl.ds(start, CHUNK)]
+            token, depth_bin, cell = rows[0:1], rows[1:2], rows[2:3]
+            token_ids = lax.broadcasted_iota(jnp.int32, (tokens, CHUNK), 0)
+            pick = jnp.where(token_ids == token, 1.0, 0.0).astype(jnp.bfloat16)
+            got = jnp.dot(held[k], pick, preferred_element_type=jnp.float32)
+            bin_ids = lax.broadcasted_iota(jnp.int32, (bins, CHUNK), 0)
+            weight = jnp.sum(
+                jnp.where(bin_ids == depth_bin, got[:bins], 0.0), axis=0, keepdims=True
+            )
+            upper = cell >= half
+            low = jnp.where(upper, 0.0, weight) * got[bins:]
+            high = jnp.where(upper, weight, 0.0) * got[bins:]
+            lifted = jnp.concatenate([low, high], axis=0).astype(jnp.bfloat16)
+            local = jnp.where(upper, cell - half, cell)
+            cell_ids = lax.broadcasted_iota(jnp.int32, (half, CHUNK), 0)
+            place = jnp.where(cell_ids == local, 1.0, 0.0).astype(jnp.bfloat16)
+            out_ref[...] += lax.dot_general(
+                place, lifted, (((1,), (1,)), ((), ())), preferred_element_type=jnp.float32
+            )
+            return inner
+
+        return lax.fori_loop(0, chunks, step, carry)
+
+    lax.fori_loop(0, tiles, one_source, 0)
+    lax.fori_loop(1, tiles, finish, 0)
 
 
 def splat_cells(rows, table, cell_count, channels):
     half = cell_count // 2
+    tiles = rows.shape[0]
     out = pl.pallas_call(
         splat_kernel,
         out_shape=jax.ShapeDtypeStruct((half, 2 * channels), jnp.float32),
         in_specs=[pl.BlockSpec(memory_space=pltpu.VMEM)] * 2,
         out_specs=pl.BlockSpec(memory_space=pltpu.VMEM),
-        compiler_params=pltpu.CompilerParams(vmem_limit_bytes=48 * 1024 * 1024),
+        scratch_shapes=[
+            pltpu.VMEM((tiles, *table.shape), table.dtype),
+            pltpu.SemaphoreType.DMA((tiles,)),
+            pltpu.SemaphoreType.DMA((tiles,)),
+        ],
+        compiler_params=pltpu.CompilerParams(
+            collective_id=0, has_side_effects=True, vmem_limit_bytes=48 * 1024 * 1024
+        ),
         cost_estimate=pl.CostEstimate(
-            flops=2 * cell_count * channels * rows.shape[0] * rows.shape[2],
+            flops=2 * cell_count * channels * tiles * rows.shape[2],
             bytes_accessed=4 * cell_count * channels,
             transcendentals=0,
         ),
@@ -160,9 +210,8 @@
     depth = jax.nn.softmax(logits, axis=0)
     channels = context.shape[0]
     table = jnp.concatenate([depth, context], axis=0).astype(jnp.bfloat16)
-    table_all = lax.all_gather(table, "tile", axis=0, tiled=False)
     cell_count = SCN * ROWS_DEV * GRID_W
-    splat = splat_cells(rows, table_all, cell_count, channels)
+    splat = splat_cells(rows, table, cell_count, channels)
     bev = splat.astype(jnp.bfloat16).reshape(SCN, ROWS_DEV, GRID_W, channels)
     extended = extended_2(bev, (("tile", 1),), 2)
     middle_wide = jnp.maximum(conv_rows(extended, conv1_weight) + conv1_bias, 0.0)

time: 315 us -> 295 us (0.937)
  blocking collectives: 31.9 us -> 0 us
  Pallas kernels: 27.4 us -> 34.9 us
  starting transfers between devices: 10.8 us -> 14.1 us
    all_gather x1 -> x0, blocking collectives: 31.9 us -> none  [on_device(): table_all = lax.all_gather(table, 'tile', axis=0, tiled=False)]
    pallas_call x1, Pallas kernels: 27.4 us -> 34.9 us  [splat_cells(): pl.pallas_call(splat_kernel, out_shape=jax.ShapeDtypeStruct((half, 2 * ch...]
    ppermute x1, waiting for transfers between devices: 2.36 us -> 8.49 us  [extended_2(): before = lax.ppermute(last, axis, up)]
    ppermute x1, waiting for transfers between devices: 4.41 us -> 0.01 us  [extended_2(): after = lax.ppermute(leading, axis, down)]
    ppermute x1, starting transfers between devices: 1.93 us -> 5.28 us  [extended_2(): before = lax.ppermute(last, axis, up)]
  transfers between devices with their start and end apart: 6 -> 6, of which waited for: 6 -> 5; matrix products, arithmetic and copies ran while one was open for 3% -> 4% of each run, Pallas kernels for 0% -> 0%
where the time goes in v2:
time: 295 us
  waiting for transfers between devices  202 us (68%)
  Pallas kernels  34.9 us (12%)
  matrix products  19.3 us (7%)
  starting transfers between devices  14.1 us (5%)
  between operations  13.5 us (5%)
  other arithmetic  6.3 us (2%)
  local copies, waits for them, and re-layouts  5 us (2%)
    all_gather x1, waiting for transfers between devices, on_device(): lax.all_gather(down_weight.T, ('cam', 'tile'), axis=0, tiled=True)  68.9 us
    all_gather x1, waiting for transfers between devices, on_device(): lax.all_gather(up_weight, ('cam', 'tile'), axis=0, tiled=True)  63.7 us
    all_gather x1, waiting for transfers between devices, on_device(): lax.all_gather(gate_weight, ('cam', 'tile'), axis=0, tiled=True)  53.8 us
    pallas_call x1, Pallas kernels, splat_cells(): pl.pallas_call(splat_kernel, out_shape=jax.ShapeDtypeStruct((half, 2 * ch...  34.9 us
    ppermute x1, waiting for transfers between devices, extended_2(): before = lax.ppermute(last, axis, up)  8.49 us
    dot_general x1, matrix products, on_device(): lax.dot_general(hidden, down_whole, (((1,), (1,)), ((), ())), preferred_e...  7.89 us
    all_to_all x1, starting transfers between devices, slot_rows(): lax.all_to_all(packed, 'tile', split_axis=0, concat_axis=0, tiled=True)  7.28 us
  transfers between devices with their start and end apart: 6, of which 5 were waited for; matrix products, arithmetic and copies ran while one was open for 4% of the time, Pallas kernels for 0%

profile of v2, /device:TPU:0, one launch (start us, length us, event | category | flops | bytes accessed | tf_op | source)
XLA Modules:
  0.0 294.8 jit_solution(15668558754558991822)
XLA Ops:
  6.5 0.7 all-gather.4.cloned.1.call-update
  7.3 0.7 all-gather.6.cloned.1.call-update
  8.1 0.7 all-gather.8.cloned.1.call-update
  8.7 1.7 fusion.24
  10.5 7.3 %all-to-all-start = ((s32[8,1,2503]{2,1,0:T(1,128)}), s32[8,1,2503]{2,1,0:T(1,128)S(1)}, u32[]{:S(2)}, u32[]{:S(2)}) async-start(s32[8,1,2503]{2,1,0:T(1,128)} %fusion.24), calls=%async_computation | async-start | bytes 163840 | tf_op jit(solution)/shard_map/all_to_all | solution.py:159
  17.8 1.1 convert_reduce_fusion
  18.9 1.3 fusion.5
  20.2 4.7 %all-to-all-done = s32[8,1,2503]{2,1,0:T(1,128)S(1)} async-done(((s32[8,1,2503]{2,1,0:T(1,128)}), s32[8,1,2503]{2,1,0:T(1,128)S(1)}, u32[]{:S(2)}, u32[]{:S(2)}) %all-to-all-start) | async-done | bytes 80128 | tf_op jit(solution)/shard_map/all_to_all | solution.py:159
  25.4 1.1 stack.19.rows_ref
  26.5 53.8 %all-gather.4.cloned.1.call-done = bf16[1024,2730]{1,0:T(8,128)(2,1)} async-done(((bf16[32,2730]{1,0:T(8,128)(2,1)}), bf16[1024,2730]{1,0:T(8,128)(2,1)}) %all-gather.4.cloned.1.call-update) | async-done | bytes 5591056 | tf_op jit(solution)/shard_map/all_gather | solution.py:191
  80.3 5.2 %fusion.10 = f32[176,2730]{1,0:T(8,128)} fusion(bf16[1024,2730]{1,0:T(8,128)(2,1)} %all-gather.4.cloned.1.call-done, bf16[176,1024]{1,0:T(8,128)(2,1)S(1)} %copy-done.1, f32[1024]{0:T(1024)S(1)} %copy-done.8, f32[176]{0:T(256)S(1)} %add_rsqrt_fusion.1, f32[176]{0:T(256)S(1)} %broadcast_multiply_fusion.1), kind=kOutput, calls=%fused_computation.42 | convolution fusion | flops 984924160 | bytes 7878912 | tf_op jit(solution)/shard_map/dot_general | solution.py:194
  85.6 63.7 %all-gather.6.cloned.1.call-done = bf16[1024,2730]{1,0:T(8,128)(2,1)} async-done(((bf16[32,2730]{1,0:T(8,128)(2,1)}), bf16[1024,2730]{1,0:T(8,128)(2,1)}) %all-gather.6.cloned.1.call-update) | async-done | bytes 5591056 | tf_op jit(solution)/shard_map/all_gather | solution.py:192
  149.2 68.9 %all-gather.8.cloned.1.call-done = bf16[1024,2730]{1,0:T(8,128)(2,1)} async-done(((bf16[32,2730]{1,0:T(8,128)(2,1)}), bf16[1024,2730]{1,0:T(8,128)(2,1)}) %all-gather.8.cloned.1.call-update) | async-done | bytes 5591056 | tf_op jit(solution)/shard_map/all_gather | solution.py:197
  218.2 7.9 %fusion.73 = (f32[176]{0:T(256)S(1)}, f32[176,1024]{1,0:T(8,128)S(1)}) fusion(bf16[1024,2730]{1,0:T(8,128)(2,1)} %all-gather.8.cloned.1.call-done, bf16[1024,2730]{1,0:T(8,128)(2,1)} %all-gather.6.cloned.1.call-done, f32[176,2730]{1,0:T(8,128)} %fusion.10, bf16[176,1024]{1,0:T(8,128)(2,1)S(1)} %copy-done.1, f32[1024]{0:T(1024)S(1)} %copy-done.8, ...), kind=kOutput, calls=%fused_computation.130 | convolution fusion | flops 1972370688 | bytes 14191552 | tf_op jit(solution)/shard_map/dot_general | solution.py:198
  226.5 0.5 copy-done.4
  227.7 34.9 %shard_map.145 = f32[1024,256]{1,0:T(8,128)S(1)} custom-call(s32[8,8,2560]{2,1,0:T(8,128)S(1)} %stack.19.rows_ref, bf16[192,176]{1,0:T(8,128)(2,1)S(1)} %pad_maximum_fusion.4.table_ref), custom_call_target="tpu_custom_call" | custom-call | flops 10737418240 | bytes 1048576 | tf_op jit(solution)/shard_map/pallas_call | solution.py:132
  262.8 5.3 %collective-permute-start = (bf16[2,2,256,128]{3,2,1,0:T(8,128)(2,1)S(1)}, bf16[2,2,256,128]{3,2,1,0:T(8,128)(2,1)S(1)}, u32[]{:S(2)}, u32[]{:S(2)}) collective-permute-start(bf16[2,2,256,128]{3,2,1,0:T(8,128)(2,1)S(1)} %get-tuple-element.23), channel_id=1, source_target_pairs={{0,1},{1,2},{2,3},{3,4},{4,5},{5,6},{6,7},{8,9},{9,10},{10,11},{11... | collective-permute-start | bytes 786440 | tf_op jit(solution)/shard_map/ppermute | solution.py:20
  268.1 1.5 collective-permute-start.1
  269.6 8.5 %collective-permute-done = bf16[2,2,256,128]{3,2,1,0:T(8,128)(2,1)S(1)} collective-permute-done((bf16[2,2,256,128]{3,2,1,0:T(8,128)(2,1)S(1)}, bf16[2,2,256,128]{3,2,1,0:T(8,128)(2,1)S(1)}, u32[]{:S(2)}, u32[]{:S(2)}) %collective-permute-start) | collective-permute-done | bytes 262176 | tf_op jit(solution)/shard_map/ppermute | solution.py:20
  278.2 1.3 pad_slice_fusion.1
  282.5 0.4 fusion.1
  283.4 1.0 pad_slice_fusion.6
  287.0 0.4 copy-done.6
  287.3 0.9 add_convert_fusion
  (64 shorter events, 7.9 us)
Async XLA Ops:
  6.5 220.8 %copy-start = (bf16[1024,128]{1,0:T(8,128)(2,1)S(1)}, bf16[1024,128]{1,0:T(8,128)(2,1)}, u32[]{:S(2)}) copy-start(bf16[1024,128]{1,0:T(8,128)(2,1)} %param.22) | copy-start | bytes 786436
  6.5 73.8 %all-gather.4.cloned.1.call-start = ((), (), s32[]{:S(2)}) async-start(), calls=%async_computation.1 | async-start | bytes 5947392 | tf_op jit(solution)/shard_map/all_gather | solution.py:191
  7.3 142.0 %all-gather.6.cloned.1.call-start = ((), (), s32[]{:S(2)}) async-start(), calls=%async_computation.2 | async-start | bytes 5947392 | tf_op jit(solution)/shard_map/all_gather | solution.py:192
  8.0 210.2 %all-gather.8.cloned.1.call-start = ((), (), s32[]{:S(2)}) async-start(), calls=%async_computation.3 | async-start | bytes 5947392 | tf_op jit(solution)/shard_map/all_gather | solution.py:197
  10.5 14.4 %all-to-all-start = ((s32[8,1,2503]{2,1,0:T(1,128)}), s32[8,1,2503]{2,1,0:T(1,128)S(1)}, u32[]{:S(2)}, u32[]{:S(2)}) async-start(s32[8,1,2503]{2,1,0:T(1,128)} %fusion.24), calls=%async_computation | async-start | bytes 163840 | tf_op jit(solution)/shard_map/all_to_all | solution.py:159
  18.9 61.5 %copy-start.1 = (bf16[176,1024]{1,0:T(8,128)(2,1)S(1)}, bf16[176,1024]{1,0:T(8,128)(2,1)}, u32[]{:S(2)}) copy-start(bf16[176,1024]{1,0:T(8,128)(2,1)} %param.15) | copy-start | bytes 1081348
  18.9 61.5 %copy-start.8 = (f32[1024]{0:T(1024)S(1)}, f32[1024]{0:T(1024)}, u32[]{:S(2)}) copy-start(f32[1024]{0:T(1024)} %param.16) | copy-start | bytes 12292
  85.6 140.7 %copy-start.5 = (f32[1024]{0:T(1024)S(1)}, f32[1024]{0:T(1024)}, u32[]{:S(2)}) copy-start(f32[1024]{0:T(1024)} %param.20) | copy-start | bytes 12292
  226.0 0.9 copy-start.4
  262.8 15.3 %collective-permute-start = (bf16[2,2,256,128]{3,2,1,0:T(8,128)(2,1)S(1)}, bf16[2,2,256,128]{3,2,1,0:T(8,128)(2,1)S(1)}, u32[]{:S(2)}, u32[]{:S(2)}) collective-permute-start(bf16[2,2,256,128]{3,2,1,0:T(8,128)(2,1)S(1)} %get-tuple-element.23), channel_id=1, source_target_pairs={{0,1},{1,2},{2,3},{3,4},{4,5},{5,6},{6,7},{8,9},{9,10},{10,11},{11... | collective-permute-start | bytes 786440 | tf_op jit(solution)/shard_map/ppermute | solution.py:20
  268.1 10.0 %collective-permute-start.1 = (bf16[2,2,256,128]{3,2,1,0:T(8,128)(2,1)S(1)}, bf16[2,2,256,128]{3,2,1,0:T(8,128)(2,1)S(1)}, u32[]{:S(2)}, u32[]{:S(2)}) collective-permute-start(bf16[2,2,256,128]{3,2,1,0:T(8,128)(2,1)S(1)} %get-tuple-element.24), channel_id=1, source_target_pairs={{1,0},{2,1},{3,2},{4,3},{5,4},{6,5},{7,6},{9,8},{10,9},{11,10},{12... | collective-permute-start | bytes 786440 | tf_op jit(solution)/shard_map/ppermute | solution.py:21
  278.2 1.3 copy-start.2
  282.5 0.7 copy-start.7
  283.4 1.0 copy-start.3
  286.7 0.7 copy-start.6
Sparse Core Ops, SparseCore 0:
  10.2 70.0 all-gather.3
  83.2 65.9 all-gather.5
  152.2 65.9 all-gather.7
